TPU v7x, 128 devices: a whole 4x4x4 slice. The times are simulated.
128 devices in a mesh: dp: 4 (over x), space: 32 (over y, z, core).
Axes of the slice: x: 4, y: 4, z: 4, core: 2. Of those that a mesh axis runs over, the one named last changes fastest.
Arguments:
- fields: bfloat16 [4, 256, 64, 4096], P('dp', 'space'), may hold values from -6 to 6
- cotangent: bfloat16 [4, 256, 64, 4096], P('dp', 'space'), may hold values from -6 to 6
- mode_weight: bfloat16 [128, 64, 64, 128], P('space'), may hold values from -4 to 4
- mix_weight: bfloat16 [64, 64], replicated, may hold values from -0.75 to 0.75
Outputs:
- response: bfloat16 [4, 256, 64, 4096], P('dp', 'space')
- field_grad: bfloat16 [4, 256, 64, 4096], P('dp', 'space')
- mode_grad: float32 [128, 64, 64, 128], P('space', 'dp')
All inputs are finite; a program needn't handle non-finite values.
Results may differ from a plain program's by a relative error of at most 0.035.
Values may be sent and summed in bfloat16 or wider, within the bound.
No kernel may reach another device: no remote copies, remote signals or barrier semaphores. Data moves between devices by JAX's collectives and lax.ppermute only.
A program may use at most 128 MiB of HBM per device.

v0:
```python
import math
import jax
import jax.numpy as jnp
from jax import lax
from jax.sharding import PartitionSpec as P

GELU_CUBIC = 0.044715
GELU_SCALE = math.sqrt(2.0 / math.pi)


def gelu_value(values):
    inner_arg = GELU_SCALE * (values + GELU_CUBIC * values * values * values)
    return 0.5 * values * (1.0 + jnp.tanh(inner_arg))


def gelu_slope(values):
    tangent = jnp.tanh(GELU_SCALE * (values + GELU_CUBIC * values * values * values))
    return 0.5 * (1.0 + tangent) + 0.5 * values * (1.0 - tangent * tangent) * GELU_SCALE * (
        1.0 + 3.0 * GELU_CUBIC * values * values
    )


def column_angles(length, mode_count):
    positions = lax.iota(jnp.int32, length)
    frequencies = lax.iota(jnp.int32, mode_count)
    phase_index = positions[:, None] * frequencies[None, :] % length
    return phase_index.astype(jnp.float32) * (2.0 * math.pi / length)


def column_factor(mode_count):
    frequencies = lax.iota(jnp.int32, mode_count)
    single = jnp.where(frequencies == 0, 1.0, 2.0).astype(jnp.bfloat16)
    return jnp.concatenate([single, single], axis=0)


def forward_table(length, mode_count, weighted):
    angles = column_angles(length, mode_count)
    norm_scale = 1.0 / math.sqrt(length)
    table_out = jnp.concatenate(
        [jnp.cos(angles) * norm_scale, -jnp.sin(angles) * norm_scale], axis=1
    ).astype(jnp.bfloat16)
    if weighted:
        table_out = table_out * column_factor(mode_count)[None, :]
    return table_out


def inverse_table(length, mode_count, weighted):
    angles = column_angles(length, mode_count).T
    norm_scale = 1.0 / math.sqrt(length)
    table_out = jnp.concatenate(
        [jnp.cos(angles) * norm_scale, -jnp.sin(angles) * norm_scale], axis=0
    ).astype(jnp.bfloat16)
    if weighted:
        table_out = table_out * column_factor(mode_count)[:, None]
    return table_out


def row_tables(extent, mode_count, offset, length):
    slot_index = lax.iota(jnp.int32, mode_count)
    frequencies = jnp.where(
        slot_index < mode_count // 2, slot_index, extent - mode_count + slot_index
    )
    rows_here = offset + lax.iota(jnp.int32, length)
    phase_index = frequencies[:, None] * rows_here[None, :] % extent
    angles = phase_index.astype(jnp.float32) * (2.0 * math.pi / extent)
    norm_scale = 1.0 / math.sqrt(extent)
    return (
        (jnp.cos(angles) * norm_scale).astype(jnp.bfloat16),
        (jnp.sin(angles) * norm_scale).astype(jnp.bfloat16),
    )


def row_forward(cos_table, sin_table, columns):
    cos_part = jnp.einsum("kr,rcpy->ykpc", cos_table, columns, preferred_element_type=jnp.float32)
    sin_part = jnp.einsum("kr,rcpy->ykpc", sin_table, columns, preferred_element_type=jnp.float32)
    real_part = cos_part[:, :, 0] + sin_part[:, :, 1]
    imag_part = cos_part[:, :, 1] - sin_part[:, :, 0]
    return jnp.concatenate([real_part, imag_part], axis=-1)


def row_inverse(cos_table, sin_table, spectrum):
    channels = spectrum.shape[2] // 2
    cos_part = jnp.einsum("kr,ykd->rdy", cos_table, spectrum, preferred_element_type=jnp.float32)
    sin_part = jnp.einsum("kr,ykd->rdy", sin_table, spectrum, preferred_element_type=jnp.float32)
    real_part = cos_part[:, :channels] - sin_part[:, channels:]
    imag_part = cos_part[:, channels:] + sin_part[:, :channels]
    return jnp.stack([real_part, imag_part], axis=2)


def mix_modes(spectrum, weight):
    channels = weight.shape[2]
    real_prod = jnp.einsum(
        "ykc,ykcd->ykd", spectrum[..., :channels], weight, preferred_element_type=jnp.float32
    )
    imag_prod = jnp.einsum(
        "ykc,ykcd->ykd", spectrum[..., channels:], weight, preferred_element_type=jnp.float32
    )
    return jnp.concatenate(
        [
            real_prod[..., :channels] - imag_prod[..., channels:],
            real_prod[..., channels:] + imag_prod[..., :channels],
        ],
        axis=-1,
    )


def mix_adjoint(delta_modes, weight):
    channels = weight.shape[2]
    swapped = jnp.concatenate([delta_modes[..., channels:], -delta_modes[..., :channels]], axis=-1)
    first_half = jnp.einsum(
        "ykd,ykcd->ykc", delta_modes, weight, preferred_element_type=jnp.float32
    )
    second_half = jnp.einsum("ykd,ykcd->ykc", swapped, weight, preferred_element_type=jnp.float32)
    return jnp.concatenate([first_half, second_half], axis=-1)


def weight_grad(spectrum, delta_modes):
    channels = spectrum.shape[2] // 2
    swapped = jnp.concatenate([delta_modes[..., channels:], -delta_modes[..., :channels]], axis=-1)
    real_term = jnp.einsum(
        "ykc,ykd->ykcd", spectrum[..., :channels], delta_modes, preferred_element_type=jnp.float32
    )
    imag_term = jnp.einsum(
        "ykc,ykd->ykcd", spectrum[..., channels:], swapped, preferred_element_type=jnp.float32
    )
    return real_term + imag_term


def on_device(fields, cotangent, mode_weight, mix_weight):
    signal = fields[0]
    upstream = cotangent[0]
    rows_here, channels, length = signal.shape
    mode_rows = mode_weight.shape[0]
    kx_count = mode_weight.shape[1]
    groups = lax.axis_size("space")
    ky_count = mode_rows * groups
    extent = rows_here * groups
    forward_cols = forward_table(length, ky_count, False)
    weighted_cols = forward_table(length, ky_count, True)
    inverse_cols = inverse_table(length, ky_count, True)
    plain_inverse = inverse_table(length, ky_count, False)
    offset = lax.axis_index("space") * rows_here
    local_cos, local_sin = row_tables(extent, kx_count, offset, rows_here)

    def to_modes(columns):
        return lax.psum_scatter(
            row_forward(local_cos, local_sin, columns).astype(jnp.bfloat16),
            "space",
            scatter_dimension=0,
            tiled=True,
        )

    def to_rows(spectrum):
        return row_inverse(
            local_cos, local_sin, lax.all_gather(spectrum, "space", axis=0, tiled=True)
        ).astype(jnp.bfloat16)

    columns = jnp.dot(
        signal.reshape(rows_here * channels, length),
        forward_cols,
        preferred_element_type=jnp.float32,
    )
    columns = columns.astype(jnp.bfloat16).reshape(rows_here, channels, 2, ky_count)
    spectrum = to_modes(columns)
    modes_out = mix_modes(spectrum, mode_weight).astype(jnp.bfloat16)
    back_columns = to_rows(modes_out)
    spectral = jnp.dot(
        back_columns.reshape(rows_here * channels, 2 * ky_count),
        inverse_cols,
        preferred_element_type=jnp.float32,
    )
    spectral = spectral.reshape(rows_here, channels, length)
    preact = spectral + jnp.einsum(
        "rcn,cd->rdn", signal, mix_weight, preferred_element_type=jnp.float32
    )
    response = gelu_value(preact).astype(jnp.bfloat16)
    delta_field = (upstream.astype(jnp.float32) * gelu_slope(preact)).astype(jnp.bfloat16)
    delta_cols = jnp.dot(
        delta_field.reshape(rows_here * channels, length),
        weighted_cols,
        preferred_element_type=jnp.float32,
    )
    delta_cols = delta_cols.astype(jnp.bfloat16).reshape(rows_here, channels, 2, ky_count)
    delta_modes = to_modes(delta_cols)
    input_modes = mix_adjoint(delta_modes, mode_weight).astype(jnp.bfloat16)
    grad_local = weight_grad(spectrum, delta_modes)
    mode_grad = lax.psum_scatter(
        grad_local.astype(jnp.bfloat16), "dp", scatter_dimension=1, tiled=True
    ).astype(jnp.float32)
    input_cols = to_rows(input_modes)
    field_grad = jnp.dot(
        input_cols.reshape(rows_here * channels, 2 * ky_count),
        plain_inverse,
        preferred_element_type=jnp.float32,
    )
    field_grad = field_grad.reshape(rows_here, channels, length)
    field_grad = field_grad + jnp.einsum(
        "rdn,cd->rcn", delta_field, mix_weight, preferred_element_type=jnp.float32
    )
    return (response[None], field_grad.astype(jnp.bfloat16)[None], mode_grad)


def solution(mesh):
    in_specs = (
        P("dp", "space", None, None),
        P("dp", "space", None, None),
        P("space", None, None, None),
        P(),
    )
    out_specs = (
        P("dp", "space", None, None),
        P("dp", "space", None, None),
        P("space", "dp", None, None),
    )
    return jax.shard_map(
        on_device, mesh=mesh, in_specs=in_specs, out_specs=out_specs, check_vma=False
    )
```

profile of v0, /device:TPU:1, one launch (start us, length us, event | category | flops | bytes accessed | tf_op | source)
XLA Modules:
  0.0 377.6 jit_solution(5238253479102441029)
XLA Ops:
  7.2 8.6 %multiply_convert_fusion.3 = (bf16[4096,128]{1,0:T(8,128)(2,1)S(1)}, bf16[4096,128]{1,0:T(8,128)(2,1)S(1)}) fusion(), kind=kLoop, calls=%fused_computation.61 | loop fusion | flops 9961472 | bytes 2097152 | tf_op jit(solution)/shard_map/convert.28
  15.9 3.9 %fusion.41 = bf16[512,256]{0,1:T(8,128)(2,1)S(1)} fusion(bf16[512,4096]{1,0:T(8,128)(2,1)} %bitcast.175, bf16[4096,128]{1,0:T(8,128)(2,1)S(1)} %get-tuple-element.19, bf16[4096,128]{1,0:T(8,128)(2,1)S(1)} %get-tuple-element.20), kind=kOutput, calls=%fused_computation.74 | convolution fusion | flops 1078067200 | bytes 6553600 | tf_op jit(solution)/shard_map/dot_general | solution.py:158
  20.0 0.9 convolution_bitcast_fusion.2
  20.9 0.9 convolution_bitcast_fusion.3
  21.7 0.5 fusion.43
  22.2 0.5 fusion.42
  22.9 3.3 copy.48
  26.2 80.8 %reduce-scatter.7.cloned.1.call-done = bf16[4,64,128]{2,1,0:T(8,128)(2,1)} async-done(((bf16[128,64,128]{2,1,0:T(8,128)(2,1)}), bf16[4,64,128]{2,1,0:T(8,128)(2,1)}) %reduce-scatter.7.cloned.1.call-update) | async-done | bytes 65552 | tf_op jit(solution)/shard_map/reduce_scatter | solution.py:146
  107.0 1.1 slice_convert_fusion.1
  108.1 3.6 fusion.68
  111.7 1.2 fusion.70
  113.0 0.7 pad_maximum_fusion.14
  114.0 8.5 %multiply_convert_fusion.1 = (bf16[128,4096]{1,0:T(8,128)(2,1)S(1)}, bf16[128,4096]{1,0:T(8,128)(2,1)S(1)}) fusion(), kind=kLoop, calls=%fused_computation.57 | loop fusion | flops 9961472 | bytes 2097152 | tf_op jit(solution)/shard_map/convert.16
  122.6 36.6 %all-gather.3.cloned.1.call-done = bf16[128,64,128]{2,1,0:T(8,128)(2,1)} async-done(((bf16[4,64,128]{2,1,0:T(8,128)(2,1)}), bf16[128,64,128]{2,1,0:T(8,128)(2,1)}) %all-gather.3.cloned.1.call-update) | async-done | bytes 2097168 | tf_op jit(solution)/shard_map/all_gather | solution.py:155
  159.2 2.1 convolution_bitcast_fusion.6
  161.3 2.1 convolution_bitcast_fusion.7
  163.4 0.3 fusion.54
  163.9 1.4 fusion.25
  165.3 0.8 copy-done.6
  166.1 1.3 copy-done.7
  167.3 8.5 %fusion.6 = (bf16[8,64,4096]{2,1,0:T(8,128)(2,1)S(1)}, bf16[1,8,64,4096]{3,2,1,0:T(8,128)(2,1)}) fusion(bf16[1,8,64,4096]{3,2,1,0:T(8,128)(2,1)S(1)} %copy-done.6, f32[8,64,4096]{2,1,0:T(8,128)S(1)} %fusion.25, bf16[1,8,64,4096]{3,2,1,0:T(8,128)(2,1)S(1)} %copy-done.7, bf16[64,64]{1,0:T(8,128)(2,1)S(1)} %copy-done), kind=kOutput, calls=%fused_computation.8 | convolution fusion | flops 316669952 | bytes 25174016 | tf_op jit(solution)/shard_map/rcn,cd->rdn/dot_general | solution.py:173
  175.8 2.0 copy-done.1
  177.8 2.0 fusion.38
  179.8 1.0 reshape.53
  180.8 0.9 convolution_bitcast_fusion
  181.7 0.9 convolution_bitcast_fusion.1
  182.6 0.5 fusion.45
  183.0 0.5 fusion.44
  183.5 1.5 pad_maximum_fusion.3
  185.0 4.6 %copy.56 = bf16[128,64,128]{2,1,0:T(8,128)(2,1)} copy(bf16[128,64,128]{0,1,2:T(8,128)(2,1)} %pad_maximum_fusion.3) | data formatting | bytes 4194304 | tf_op jit(solution)/shard_map/concatenate | solution.py:78
  189.8 76.1 %reduce-scatter.9.cloned.1.call-done = bf16[4,64,128]{2,1,0:T(8,128)(2,1)} async-done(((bf16[128,64,128]{2,1,0:T(8,128)(2,1)}), bf16[4,64,128]{2,1,0:T(8,128)(2,1)}) %reduce-scatter.9.cloned.1.call-update) | async-done | bytes 65552 | tf_op jit(solution)/shard_map/reduce_scatter | solution.py:146
  266.0 1.1 fusion.132
  267.2 4.6 %fusion.64 = f32[4,64,1,64]{3,2,1,0:T(1,128)S(1)} fusion(bf16[4,64,64,128]{3,2,1,0:T(8,128)(2,1)} %param.6, bf16[4,64,128,1]{2,1,0,3:T(8,128)(2,1)S(1)} %get-tuple-element.12), kind=kOutput, calls=%fused_computation.106 | convolution fusion | flops 4194304 | bytes 4325376 | tf_op jit(solution)/shard_map/ykd,ykcd->ykc/dot_general | solution.py:113
  271.8 2.3 fusion.66
  274.1 0.7 pad_maximum_fusion.16
  275.0 5.4 %add_convert_fusion = bf16[4,64,64,128]{3,2,1,0:T(8,128)(2,1)S(1)} fusion(f32[4,64,128]{2,1,0:T(8,128)S(1)} %get-tuple-element.11, f32[4,64,64]{2,1,0:T(8,128)S(1)} %get-tuple-element.14, f32[4,64,128]{2,1,0:T(8,128)S(1)} %convert.86, f32[4,64,64]{2,1,0:T(8,128)S(1)} %get-tuple-element.13), kind=kLoop, calls=%fused_computation.12 | loop fusion | flops 8388608 | bytes 4587520 | tf_op jit(solution)/shard_map/convert_element_type | solution.py:188
  280.4 1.4 copy.75
  281.8 4.8 %copy.103 = bf16[8,8,256,128]{3,1,2,0:T(8,128)(2,1)} copy(bf16[8,8,256,128]{3,2,1,0:T(8,128)(2,1)S(1)} %bitcast.164) | data formatting | bytes 8388608
  286.6 33.6 %all-gather.5.cloned.1.call-done = bf16[128,64,128]{2,1,0:T(8,128)(2,1)} async-done(((bf16[4,64,128]{2,1,0:T(8,128)(2,1)}), bf16[128,64,128]{2,1,0:T(8,128)(2,1)}) %all-gather.5.cloned.1.call-update) | async-done | bytes 2097168 | tf_op jit(solution)/shard_map/all_gather | solution.py:155
  320.2 2.1 convolution_bitcast_fusion.4
  322.3 2.1 convolution_bitcast_fusion.5
  324.4 0.3 fusion.56
  324.9 1.3 fusion.23
  326.2 0.9 copy-done.2
  327.1 3.3 fusion.8
  330.3 37.8 %reduce-scatter.11.cloned.1.call-done = bf16[16,32768]{1,0:T(8,128)(2,1)} async-done(((bf16[64,32768]{1,0:T(8,128)(2,1)}), bf16[16,32768]{1,0:T(8,128)(2,1)}) %reduce-scatter.11.cloned.1.call-update) | async-done | bytes 1048592
  368.1 1.4 copy.80
  369.5 1.6 copy_convert_fusion
  (40 shorter events, 1.7 us)
Async XLA Ops:
  7.2 158.1 %copy-start = (bf16[64,64]{1,0:T(8,128)(2,1)S(1)}, bf16[64,64]{1,0:T(8,128)(2,1)}, u32[]{:S(2)}) copy-start(bf16[64,64]{1,0:T(8,128)(2,1)} %param.7) | copy-start | bytes 24580
  7.2 99.8 %reduce-scatter.7.cloned.1.call-start = ((), (), s32[]{:S(2)}) async-start(), calls=%async_computation.3 | async-start | bytes 2162688 | tf_op jit(solution)/shard_map/reduce_scatter | solution.py:146
  15.9 3.9 %copy-start.3 = (bf16[4096,128]{1,0:T(8,128)(2,1)}, bf16[4096,128]{1,0:T(8,128)(2,1)S(1)}, u32[]{:S(2)}) copy-start(bf16[4096,128]{1,0:T(8,128)(2,1)S(1)} %get-tuple-element.20) | copy-start | bytes 3145732
  26.2 133.0 %all-gather.3.cloned.1.call-start = ((), (), s32[]{:S(2)}) async-start(), calls=%async_computation.4 | async-start | bytes 2162688 | tf_op jit(solution)/shard_map/all_gather | solution.py:155
  107.0 4.7 %copy-start.8 = (bf16[4,64,64,128]{3,2,1,0:T(8,128)(2,1)S(1)}, bf16[4,64,64,128]{3,2,1,0:T(8,128)(2,1)}, u32[]{:S(2)}) copy-start(bf16[4,64,64,128]{3,2,1,0:T(8,128)(2,1)} %param.6) | copy-start | bytes 12582916
  113.8 152.2 %reduce-scatter.9.cloned.1.call-start = ((), (), s32[]{:S(2)}) async-start(), calls=%async_computation.5 | async-start | bytes 2162688 | tf_op jit(solution)/shard_map/reduce_scatter | solution.py:146
  163.9 2.2 copy-start.6
  163.9 3.5 copy-start.7
  167.3 10.5 %copy-start.4 = (bf16[4096,128]{1,0:T(8,128)(2,1)S(1)}, bf16[4096,128]{1,0:T(8,128)(2,1)}, u32[]{:S(2)}) copy-start(bf16[4096,128]{1,0:T(8,128)(2,1)} %copy-done.3) | copy-start | bytes 3145732
  175.8 2.0 copy-start.1
  189.6 130.6 %all-gather.5.cloned.1.call-start = ((), (), s32[]{:S(2)}) async-start(), calls=%async_computation.6 | async-start | bytes 2162688 | tf_op jit(solution)/shard_map/all_gather | solution.py:155
  266.0 5.8 %copy-start.5 = (bf16[4,64,128]{2,1,0:T(8,128)(2,1)S(1)}, bf16[4,64,128]{2,1,0:T(8,128)(2,1)}, u32[]{:S(2)}) copy-start(bf16[4,64,128]{2,1,0:T(8,128)(2,1)} %reduce-scatter.9.cloned.1.call-done) | copy-start | bytes 196612
  266.0 5.8 %copy-start.9 = (bf16[4,64,64,128]{3,2,1,0:T(8,128)(2,1)S(1)}, bf16[4,64,64,128]{3,2,1,0:T(8,128)(2,1)}, u32[]{:S(2)}) copy-start(bf16[4,64,64,128]{3,2,1,0:T(8,128)(2,1)} %param.6) | copy-start | bytes 12582916
  274.9 93.3 %reduce-scatter.11.cloned.1.call-start = ((), (), s32[]{:S(2)}) async-start(), calls=%async_computation.7 | async-start | bytes 5242880
  324.9 2.2 copy-start.2
Sparse Core Ops, SparseCore 0:
  26.3 80.6 reduce-scatter.6
  113.9 45.2 all-gather.2
  189.7 76.2 reduce-scatter.8
  275.0 45.1 all-gather.4
  322.5 45.6 reduce-scatter.10
where the time goes:
time: 378 us
  waiting for transfers between devices  265 us (70%)
  matrix products  43.6 us (12%)
  other arithmetic  32.6 us (9%)
  local copies, waits for them, and re-layouts  21.7 us (6%)
  between operations  14.1 us (4%)
    reduce_scatter x2, waiting for transfers between devices, to_modes(): lax.psum_scatter(row_forward(local_cos, local_sin, columns).astype(jnp.bf...  157 us
    all_gather x2, waiting for transfers between devices, to_rows(): lax.all_gather(spectrum, 'space', axis=0, tiled=True)  70.3 us
    unnamed x6, waiting for transfers between devices  37.9 us
    another operation x8, other arithmetic  18.6 us
    unnamed x23, local copies, waits for them, and re-layouts  12.6 us
    dot_general x1, matrix products, on_device(): jnp.einsum('rcn,cd->rdn', signal, mix_weight, preferred_element_type=jnp....  8.47 us
    concatenate x2, local copies, waits for them, and re-layouts, row_forward(): return jnp.concatenate([real_part, imag_part], axis=-1)  7.85 us
  transfers between devices with their start and end apart: 5, of which 5 were waited for; matrix products, arithmetic and copies ran while one was open for 8% of the time, Pallas kernels for 0%

commit v1 on v0

--- a/solution.py
+++ b/solution.py
@@ -152,7 +152,12 @@
 
     def to_rows(spectrum):
         return row_inverse(
-            local_cos, local_sin, lax.all_gather(spectrum, "space", axis=0, tiled=True)
+            local_cos,
+            local_sin,
+            jnp.concatenate(
+                lax.all_to_all(jnp.stack([spectrum] * lax.axis_size("space")), "space", 0, 0),
+                axis=0,
+            ),
         ).astype(jnp.bfloat16)
 
     columns = jnp.dot(

time: 378 us -> 323 us (0.85)
  waiting for transfers between devices: 265 us -> 174 us
  blocking collectives: 0 us -> 35.2 us
  matrix products: 43.6 us -> 36.3 us
  starting transfers between devices: 0.61 us -> 7.81 us
    all_gather x2 -> x0, waiting for transfers between devices: 70.3 us -> none  [to_rows(): lax.all_gather(spectrum, 'space', axis=0, tiled=True)]
    unnamed x6 -> x4, waiting for transfers between devices: 37.9 us -> 0.05 us
    all_to_all x0 -> x1, blocking collectives: none -> 35.2 us  [to_rows(): lax.all_to_all(jnp.stack([spectrum] * lax.axis_size('space')), 'space', 0...]
    all_to_all x0 -> x1, waiting for transfers between devices: none -> 18.8 us  [to_rows(): lax.all_to_all(jnp.stack([spectrum] * lax.axis_size('space')), 'space', 0...]
    all_to_all x0 -> x1, starting transfers between devices: none -> 7.29 us  [to_rows(): lax.all_to_all(jnp.stack([spectrum] * lax.axis_size('space')), 'space', 0...]
    unnamed x23 -> x31, local copies, waits for them, and re-layouts: 12.6 us -> 13.9 us
  transfers between devices with their start and end apart: 5 -> 4, of which waited for: 5 -> 3; matrix products, arithmetic and copies ran while one was open for 8% -> 7% of each run, Pallas kernels for 0% -> 0%
where the time goes in v1:
time: 323 us; the launch traced here: 322 us
  waiting for transfers between devices  174 us (54%)
  matrix products  36.3 us (11%)
  blocking collectives  35.2 us (11%)
  other arithmetic  31.4 us (10%)
  local copies, waits for them, and re-layouts  23.1 us (7%)
  between operations  14.1 us (4%)
  starting transfers between devices  7.81 us (2%)
    reduce_scatter x2, waiting for transfers between devices, to_modes(): lax.psum_scatter(row_forward(local_cos, local_sin, columns).astype(jnp.bf...  155 us
    all_to_all x1, blocking collectives, to_rows(): lax.all_to_all(jnp.stack([spectrum] * lax.axis_size('space')), 'space', 0...  35.2 us
    another operation x8, other arithmetic  20.1 us
    all_to_all x1, waiting for transfers between devices, to_rows(): lax.all_to_all(jnp.stack([spectrum] * lax.axis_size('space')), 'space', 0...  18.8 us
    unnamed x31, local copies, waits for them, and re-layouts  13.9 us
    dot_general x1, matrix products, on_device(): jnp.einsum('rcn,cd->rdn', signal, mix_weight, preferred_element_type=jnp....  8.46 us
    all_to_all x1, starting transfers between devices, to_rows(): lax.all_to_all(jnp.stack([spectrum] * lax.axis_size('space')), 'space', 0...  7.29 us
    concatenate x2, local copies, waits for them, and re-layouts, row_forward(): return jnp.concatenate([real_part, imag_part], axis=-1)  6.57 us
  transfers between devices with their start and end apart: 4, of which 3 were waited for; matrix products, arithmetic and copies ran while one was open for 7% of the time, Pallas kernels for 0%

profile of v1, /device:TPU:1, one launch (start us, length us, event | category | flops | bytes accessed | tf_op | source)
XLA Modules:
  0.0 322.2 jit_solution(837566217099978579)
XLA Ops:
  7.2 8.6 %multiply_convert_fusion.3 = (bf16[4096,128]{1,0:T(8,128)(2,1)S(1)}, bf16[4096,128]{1,0:T(8,128)(2,1)S(1)}) fusion(), kind=kLoop, calls=%fused_computation.61 | loop fusion | flops 9961472 | bytes 2097152 | tf_op jit(solution)/shard_map/convert.28
  15.9 1.0 copy-done.5
  17.2 3.5 %fusion.41 = bf16[512,256]{0,1:T(8,128)(2,1)S(1)} fusion(bf16[512,4096]{1,0:T(8,128)(2,1)} %bitcast.181, bf16[4096,128]{1,0:T(8,128)(2,1)S(1)} %get-tuple-element.19, bf16[4096,128]{1,0:T(8,128)(2,1)S(1)} %get-tuple-element.20), kind=kOutput, calls=%fused_computation.74 | convolution fusion | flops 1078067200 | bytes 6553600 | tf_op jit(solution)/shard_map/dot_general | solution.py:163
  21.0 0.9 convolution_bitcast_fusion.2
  21.9 0.9 convolution_bitcast_fusion.3
  22.7 0.5 fusion.43
  23.2 0.5 fusion.42
  23.9 3.3 %copy.48 = bf16[128,64,128]{2,1,0:T(8,128)(2,1)} copy(bf16[128,64,128]{0,1,2:T(8,128)(2,1)S(1)} %pad_maximum_fusion.1) | data formatting | bytes 4194304 | tf_op jit(solution)/shard_map/concatenate | solution.py:78
  27.2 80.7 %reduce-scatter.7.cloned.1.call-done = bf16[4,64,128]{2,1,0:T(8,128)(2,1)} async-done(((bf16[128,64,128]{2,1,0:T(8,128)(2,1)}), bf16[4,64,128]{2,1,0:T(8,128)(2,1)}) %reduce-scatter.7.cloned.1.call-update) | async-done | bytes 65552 | tf_op jit(solution)/shard_map/reduce_scatter | solution.py:146
  107.9 1.1 slice_convert_fusion.1
  109.0 3.6 %fusion.68 = f32[4,64,1,128]{3,2,1,0:T(1,128)S(1)} fusion(bf16[4,64,64,128]{3,2,1,0:T(8,128)(2,1)} %param.6, bf16[4,64,64,1]{2,1,0,3:T(8,128)(2,1)S(1)} %get-tuple-element.15), kind=kOutput, calls=%fused_computation.110 | convolution fusion | flops 4194304 | bytes 4358144 | tf_op jit(solution)/shard_map/ykc,ykcd->ykd/dot_general | solution.py:95
  112.6 1.2 fusion.70
  114.0 1.8 stack.22
  115.9 7.3 %all-to-all-start = ((bf16[32,4,64,128]{3,2,1,0:T(8,128)(2,1)}), bf16[32,4,64,128]{3,2,1,0:T(8,128)(2,1)S(1)}, u32[]{:S(2)}, u32[]{:S(2)}) async-start(bf16[32,4,64,128]{3,2,1,0:T(8,128)(2,1)} %stack.22), calls=%async_computation.1 | async-start | bytes 4194304 | tf_op jit(solution)/shard_map/all_to_all | solution.py:158
  123.4 9.2 %multiply_convert_fusion.1 = (bf16[128,4096]{1,0:T(8,128)(2,1)S(1)}, bf16[128,4096]{1,0:T(8,128)(2,1)}) fusion(), kind=kLoop, calls=%fused_computation.57 | loop fusion | flops 9961472 | bytes 2097152 | tf_op jit(solution)/shard_map/convert.16
  132.6 18.8 %all-to-all-done = bf16[32,4,64,128]{3,2,1,0:T(8,128)(2,1)S(1)} async-done(((bf16[32,4,64,128]{3,2,1,0:T(8,128)(2,1)}), bf16[32,4,64,128]{3,2,1,0:T(8,128)(2,1)S(1)}, u32[]{:S(2)}, u32[]{:S(2)}) %all-to-all-start) | async-done | bytes 2097184 | tf_op jit(solution)/shard_map/all_to_all | solution.py:158
  151.5 0.5 convolution_bitcast_fusion.6
  152.0 0.5 convolution_bitcast_fusion.7
  152.5 0.3 fusion.54
  153.0 1.4 fusion.25
  154.4 0.7 copy-done.10
  155.2 1.3 copy-done.11
  156.4 8.5 %fusion.6 = (bf16[8,64,4096]{2,1,0:T(8,128)(2,1)S(1)}, bf16[1,8,64,4096]{3,2,1,0:T(8,128)(2,1)}) fusion(bf16[1,8,64,4096]{3,2,1,0:T(8,128)(2,1)S(1)} %copy-done.10, f32[8,64,4096]{2,1,0:T(8,128)S(1)} %fusion.25, bf16[1,8,64,4096]{3,2,1,0:T(8,128)(2,1)S(1)} %copy-done.11, bf16[64,64]{1,0:T(8,128)(2,1)S(1)} %copy-done), kind=kOutput, calls=%fused_computation.8 | convolution fusion | flops 316669952 | bytes 25174016 | tf_op jit(solution)/shard_map/rcn,cd->rdn/dot_general | solution.py:178
  164.9 2.0 copy-done.3
  166.9 1.3 fusion.38
  168.3 0.9 convolution_bitcast_fusion
  169.1 0.9 convolution_bitcast_fusion.1
  170.0 0.5 fusion.45
  170.5 0.5 fusion.44
  171.1 3.3 %copy.56 = bf16[128,64,128]{2,1,0:T(8,128)(2,1)} copy(bf16[128,64,128]{0,1,2:T(8,128)(2,1)S(1)} %pad_maximum_fusion.3) | data formatting | bytes 4194304 | tf_op jit(solution)/shard_map/concatenate | solution.py:78
  174.7 74.6 %reduce-scatter.9.cloned.1.call-done = bf16[4,64,128]{2,1,0:T(8,128)(2,1)} async-done(((bf16[128,64,128]{2,1,0:T(8,128)(2,1)}), bf16[4,64,128]{2,1,0:T(8,128)(2,1)}) %reduce-scatter.9.cloned.1.call-update) | async-done | bytes 65552 | tf_op jit(solution)/shard_map/reduce_scatter | solution.py:146
  249.3 1.0 fusion.132
  250.4 0.9 convert.86
  251.3 5.4 %add_convert_fusion = bf16[4,64,64,128]{3,2,1,0:T(8,128)(2,1)S(1)} fusion(f32[4,64,128]{2,1,0:T(8,128)S(1)} %get-tuple-element.11, f32[4,64,64]{2,1,0:T(8,128)S(1)} %get-tuple-element.14, f32[4,64,128]{2,1,0:T(8,128)S(1)} %convert.86, f32[4,64,64]{2,1,0:T(8,128)S(1)} %get-tuple-element.13), kind=kLoop, calls=%fused_computation.12 | loop fusion | flops 8388608 | bytes 4587520 | tf_op jit(solution)/shard_map/convert_element_type | solution.py:193
  256.7 1.4 copy.75
  258.1 4.8 %copy.103 = bf16[8,8,256,128]{3,1,2,0:T(8,128)(2,1)} copy(bf16[8,8,256,128]{3,2,1,0:T(8,128)(2,1)S(1)} %bitcast.170) | data formatting | bytes 8388608
  262.9 4.6 %fusion.64 = f32[4,64,1,64]{3,2,1,0:T(1,128)S(1)} fusion(bf16[4,64,64,128]{3,2,1,0:T(8,128)(2,1)} %param.6, bf16[4,64,128,1]{2,1,0,3:T(8,128)(2,1)S(1)} %get-tuple-element.12), kind=kOutput, calls=%fused_computation.106 | convolution fusion | flops 4194304 | bytes 4325376 | tf_op jit(solution)/shard_map/ykd,ykcd->ykc/dot_general | solution.py:113
  267.6 2.3 fusion.66
  270.0 0.5 stack.26
  270.5 35.2 %all_to_all.10 = bf16[32,4,64,128]{3,2,1,0:T(8,128)(2,1)S(1)} all-to-all(bf16[32,4,64,128]{3,2,1,0:T(8,128)(2,1)S(1)} %stack.26), channel_id=1, replica_groups=mesh['dp'=4,'space'=32] {'space'}, dimensions={0} | all-to-all | bytes 4194304 | tf_op jit(solution)/shard_map/all_to_all | solution.py:158
  305.7 0.5 convolution_bitcast_fusion.4
  306.2 0.5 convolution_bitcast_fusion.5
  306.7 0.3 fusion.56
  307.2 1.3 fusion.23
  308.5 0.9 copy-done.4
  309.5 3.2 %fusion.8 = bf16[1,8,64,4096]{3,2,1,0:T(8,128)(2,1)} fusion(f32[8,64,4096]{2,1,0:T(8,128)S(1)} %fusion.23, bf16[8,64,4096]{2,1,0:T(8,128)(2,1)S(1)} %copy-done.4, bf16[64,64]{1,0:T(8,128)(2,1)S(1)} %copy-done), kind=kOutput, calls=%fused_computation.14 | convolution fusion | flops 272629760 | bytes 16785408 | tf_op jit(solution)/shard_map/rdn,cd->rcn/dot_general | solution.py:202
  312.7 1.4 copy.80
  314.1 1.6 copy_convert_fusion
  (47 shorter events, 2.3 us)
Async XLA Ops:
  7.2 147.2 %copy-start = (bf16[64,64]{1,0:T(8,128)(2,1)S(1)}, bf16[64,64]{1,0:T(8,128)(2,1)}, u32[]{:S(2)}) copy-start(bf16[64,64]{1,0:T(8,128)(2,1)} %param.7) | copy-start | bytes 24580
  7.2 100.7 %reduce-scatter.7.cloned.1.call-start = ((), (), s32[]{:S(2)}) async-start(), calls=%async_computation.5 | async-start | bytes 2162688 | tf_op jit(solution)/shard_map/reduce_scatter | solution.py:146
  15.9 1.0 copy-start.5
  15.9 1.3 copy-start.7
  107.9 4.7 %copy-start.12 = (bf16[4,64,64,128]{3,2,1,0:T(8,128)(2,1)S(1)}, bf16[4,64,64,128]{3,2,1,0:T(8,128)(2,1)}, u32[]{:S(2)}) copy-start(bf16[4,64,64,128]{3,2,1,0:T(8,128)(2,1)} %param.6) | copy-start | bytes 12582916
  115.9 35.6 %all-to-all-start = ((bf16[32,4,64,128]{3,2,1,0:T(8,128)(2,1)}), bf16[32,4,64,128]{3,2,1,0:T(8,128)(2,1)S(1)}, u32[]{:S(2)}, u32[]{:S(2)}) async-start(bf16[32,4,64,128]{3,2,1,0:T(8,128)(2,1)} %stack.22), calls=%async_computation.1 | async-start | bytes 4194304 | tf_op jit(solution)/shard_map/all_to_all | solution.py:158
  123.2 126.1 %reduce-scatter.9.cloned.1.call-start = ((), (), s32[]{:S(2)}) async-start(), calls=%async_computation.6 | async-start | bytes 2162688 | tf_op jit(solution)/shard_map/reduce_scatter | solution.py:146
  151.5 1.5 copy-start.1
  153.0 2.2 copy-start.10
  153.0 3.5 %copy-start.11 = (bf16[1,8,64,4096]{3,2,1,0:T(8,128)(2,1)S(1)}, bf16[1,8,64,4096]{3,2,1,0:T(8,128)(2,1)}, u32[]{:S(2)}) copy-start(bf16[1,8,64,4096]{3,2,1,0:T(8,128)(2,1)} %param.4) | copy-start | bytes 12582916
  156.4 10.5 %copy-start.6 = (bf16[4096,128]{1,0:T(8,128)(2,1)S(1)}, bf16[4096,128]{1,0:T(8,128)(2,1)}, u32[]{:S(2)}) copy-start(bf16[4096,128]{1,0:T(8,128)(2,1)} %copy-done.5) | copy-start | bytes 3145732
  156.4 10.5 %copy-start.8 = (bf16[4096,128]{1,0:T(8,128)(2,1)S(1)}, bf16[4096,128]{1,0:T(8,128)(2,1)}, u32[]{:S(2)}) copy-start(bf16[4096,128]{1,0:T(8,128)(2,1)} %copy-done.7) | copy-start | bytes 3145732
  164.9 2.0 copy-start.3
  174.4 138.3 %reduce-scatter.11.cloned.1.call-start = ((), (), s32[]{:S(2)}) async-start(), calls=%async_computation.7 | async-start | bytes 5242880
  262.9 4.7 %copy-start.9 = (bf16[4,64,128]{2,1,0:T(8,128)(2,1)S(1)}, bf16[4,64,128]{2,1,0:T(8,128)(2,1)}, u32[]{:S(2)}) copy-start(bf16[4,64,128]{2,1,0:T(8,128)(2,1)} %reduce-scatter.9.cloned.1.call-done) | copy-start | bytes 196612
  262.9 4.7 %copy-start.13 = (bf16[4,64,64,128]{3,2,1,0:T(8,128)(2,1)S(1)}, bf16[4,64,64,128]{3,2,1,0:T(8,128)(2,1)}, u32[]{:S(2)}) copy-start(bf16[4,64,64,128]{3,2,1,0:T(8,128)(2,1)} %param.6) | copy-start | bytes 12582916
  305.7 1.5 copy-start.2
  307.2 2.3 copy-start.4
Sparse Core Ops, SparseCore 0:
  27.3 80.5 reduce-scatter.6
  174.6 74.7 reduce-scatter.8
  263.0 47.6 reduce-scatter.10
